TPU v7x, 512 devices: a whole 4x4x16 slice. The times are simulated.
512 devices in a mesh: dp: 64 (over y_hi, z, core), tensor: 8 (over x, y_lo).
Axes of the slice: x: 4, y: 4 (y_hi: 2, y_lo: 2; y = y_hi * 2 + y_lo), z: 16, core: 2. Of those that a mesh axis runs over, the one named last changes fastest.
Arguments:
- queries: bfloat16 [2048, 5120], P('dp', 'tensor'), may hold values from -8 to 8
- new_keys: bfloat16 [2048, 5120], P('dp', 'tensor'), may hold values from -8 to 8
- new_values: bfloat16 [2048, 5120], P('dp', 'tensor'), may hold values from -6 to 6
- key_pool: bfloat16 [1024, 16, 5120], P('dp', None, 'tensor'), may hold values from -6 to 6
- value_pool: bfloat16 [1024, 16, 5120], P('dp', None, 'tensor'), may hold values from -6 to 6
- page_table: int32 [128, 16], P('dp'), may hold values from 0 to 15, as said below
- lengths: int32 [128], P('dp'), may hold values from 1 to 240, as said below
- timesteps: int32 [128], replicated, may hold values from 0 to 49
- gate_table: float32 [50, 5120], P(None, 'dp'), may hold values from -4 to 4
- out_weight: bfloat16 [5120, 5120], P('tensor', 'dp'), may hold values from -0.078125 to 0.078125
- residual: bfloat16 [32, 64, 5120], P('tensor', None, 'dp'), may hold values from -1.5 to 1.5
Outputs:
- mixed: bfloat16 [32, 64, 5120], P('tensor', None, 'dp')
Inputs may be any that keep to these rules, and one draw needn't show every extreme that they name: `page_table`: ids of pages within the 16-page pool of the request's own group; the first ceil(lengths[r] / 16) entries of the requests of one group are distinct pages, and together they take at most 16 pages; in every draw some group takes all 16. `lengths`: some request has exactly 240 cached positions in every draw.
All inputs are finite; a program needn't handle non-finite values.
Results may differ from a plain program's by a relative error of at most 0.0054.
Values may be sent and summed in bfloat16 or wider, within the bound.
No kernel may reach another device: no remote copies, remote signals or barrier semaphores. Data moves between devices by JAX's collectives and lax.ppermute only.
A program may use at most 64 MiB of HBM per device.

v0:
```python
import math
import jax
import jax.numpy as jnp
from jax import lax
from jax.sharding import Mesh
from jax.sharding import PartitionSpec as P

HEAD = 128


def attend(queries, new_keys, new_values, key_pool, value_pool, page_table, lengths):
    req_dev = page_table.shape[0]
    pages, page_len, width = key_pool.shape
    tok_count = queries.shape[0]
    new_count = tok_count // req_dev
    heads_dev = width // HEAD
    cached = pages * page_len
    keys_all = jnp.concatenate(
        [
            key_pool[page_table].reshape(req_dev, cached, width),
            new_keys.reshape(req_dev, new_count, width),
        ],
        axis=1,
    )
    vals_all = jnp.concatenate(
        [
            value_pool[page_table].reshape(req_dev, cached, width),
            new_values.reshape(req_dev, new_count, width),
        ],
        axis=1,
    )
    keys_all = keys_all.reshape(req_dev, cached + new_count, heads_dev, HEAD)
    vals_all = vals_all.reshape(req_dev, cached + new_count, heads_dev, HEAD)
    query_four = queries.reshape(req_dev, new_count, heads_dev, HEAD)
    scores = jnp.einsum(
        "rqhd,rkhd->rhqk", query_four, keys_all, preferred_element_type=jnp.float32
    ) * (1.0 / math.sqrt(HEAD))
    position = jnp.arange(cached + new_count)
    visible = (position[None, :] < lengths[:, None]) | (position[None, :] >= cached)
    scores = jnp.where(visible[:, None, None, :], scores, jnp.float32(-1e30))
    top = jnp.max(scores, axis=-1, keepdims=True)
    expd = jnp.exp(scores - top)
    probs = (expd / jnp.sum(expd, axis=-1, keepdims=True)).astype(jnp.bfloat16)
    mixed_heads = jnp.einsum("rhqk,rkhd->rqhd", probs, vals_all, preferred_element_type=jnp.float32)
    return mixed_heads.astype(jnp.bfloat16).reshape(tok_count, width)


def per_device(
    queries,
    new_keys,
    new_values,
    key_pool,
    value_pool,
    page_table,
    lengths,
    timesteps,
    gate_table,
    out_weight,
    residual,
):
    req_dev = page_table.shape[0]
    group_tok = queries.shape[0]
    new_count = group_tok // req_dev
    share = residual.shape[0]
    groups = residual.shape[1]
    col_count = out_weight.shape[1]
    y_hi, z_len, cores = (lax.axis_size(name) for name in ("y_hi", "z", "core"))
    tensor_len = lax.axis_size("x") * lax.axis_size("y_lo")
    weight = lax.all_gather(out_weight, ("y_hi", "core"), axis=1, tiled=True)
    attn = attend(queries, new_keys, new_values, key_pool, value_pool, page_table, lengths)
    attn_all = lax.all_gather(attn, "z", axis=0, tiled=True)
    partial = jnp.dot(attn_all, weight, preferred_element_type=jnp.float32).astype(jnp.bfloat16)
    blocks = partial.reshape(z_len, tensor_len, share, y_hi * cores, col_count)
    blocks = blocks.transpose(3, 1, 0, 2, 4).reshape(-1, z_len, share, col_count)
    arrived = lax.all_to_all(blocks, ("y_hi", "core", "x", "y_lo"), 0, 0, tiled=True)
    arrived = arrived.reshape(y_hi, cores, tensor_len, z_len, share, col_count)
    branch = jnp.sum(arrived.astype(jnp.float32), axis=2)
    branch = branch.transpose(3, 0, 2, 1, 4).reshape(share, groups, col_count)
    tensor_at = lax.axis_index(("x", "y_lo"))
    local_rows = tensor_at * share + jnp.arange(share, dtype=jnp.int32)
    request_at = (
        jnp.arange(groups, dtype=jnp.int32)[None, :] * req_dev + (local_rows // new_count)[:, None]
    )
    step_at = timesteps[request_at]
    onehot = (
        step_at[:, :, None] == jnp.arange(gate_table.shape[0], dtype=jnp.int32)[None, None, :]
    ).astype(jnp.float32)
    gate = jnp.einsum("tgs,sc->tgc", onehot, gate_table, precision=lax.Precision.HIGHEST)
    return (residual.astype(jnp.float32) + gate * branch).astype(jnp.bfloat16)


def solution(mesh):
    dp = ("y_hi", "z", "core")
    tensor = ("x", "y_lo")
    split = Mesh(mesh.devices.reshape(2, -1, 2, 4, 2), dp + tensor)
    placed = (
        P(dp, tensor),
        P(dp, tensor),
        P(dp, tensor),
        P(dp, None, tensor),
        P(dp, None, tensor),
        P(dp, None),
        P(dp),
        P(),
        P(None, dp),
        P(tensor, dp),
        P(tensor, None, dp),
    )
    return jax.shard_map(
        per_device, mesh=split, in_specs=placed, out_specs=P(tensor, None, dp), check_vma=False
    )
```

profile of v0, /device:TPU:1, one launch (start us, length us, event | category | flops | bytes accessed | tf_op | source)
XLA Modules:
  0.0 78.0 jit_solution(498488600279138065)
XLA Ops:
  0.0 0.0 copy-start
  0.0 0.9 %concatenate.17 = bf16[2,16,5,128]{3,2,1,0:T(8,128)(2,1)S(1)} reshape(bf16[32,640]{1,0:T(8,128)(2,1)} %param.13) | data formatting | bytes 81920 | tf_op jit(solution)/shard_map/concatenate | solution.py:25
  0.9 0.7 compare_select_fusion.1
  1.6 0.1 reshape.161
  1.7 0.0 copy-done
  1.7 0.7 gather_fusion.1
  2.4 0.7 concatenate.16
  3.1 0.0 copy-start.5
  3.1 0.0 copy-start.2
  3.1 0.1 copy.21
  3.2 0.6 copy-done.5
  3.9 0.1 concatenate.20
  4.0 0.1 copy-done.2
  4.1 0.7 gather_fusion.2
  4.8 0.7 concatenate.19
  5.5 0.0 copy-start.6
  5.5 0.0 copy-start.8
  5.5 0.1 copy.23
  5.7 0.6 copy-done.6
  6.3 0.1 reshape.145
  6.4 0.0 copy-done.8
  6.4 0.1 compare_or_fusion
  6.5 0.5 fusion.48
  6.9 0.0 copy-start.3
  6.9 0.5 fusion.7
  7.6 33.5 %all_gather.6 = bf16[512,640]{1,0:T(8,128)(2,1)S(1)} all-gather(bf16[32,640]{1,0:T(8,128)(2,1)S(1)} %bitcast.37), channel_id=1, replica_groups=mesh['y_hi'=2,'z'=16,'core'=2,'x'=4,'y_lo'=2] {'z'}, dimensions={0}, use_global_device_ids=true | all-gather | bytes 696320 | tf_op jit(solution)/shard_map/all_gather | solution.py:71
  41.0 0.0 copy-done.3
  41.0 15.7 %all_gather.7 = bf16[640,320]{0,1:T(8,128)(2,1)S(1)} all-gather(bf16[640,80]{0,1:T(8,128)(2,1)S(1)} %copy-done.3), channel_id=1, replica_groups=mesh['y_hi'=2,'z'=16,'core'=2,'x'=4,'y_lo'=2] {'y_hi','core'}, dimensions={1}, use_global_device_ids=true | all-gather | bytes 512000 | tf_op jit(solution)/shard_map/all_gather | solution.py:69
  56.7 0.4 convolution_convert_fusion
  57.2 0.2 copy.27
  57.4 0.3 reshape.147
  57.8 0.0 copy-start.1
  57.8 1.1 %copy.28 = bf16[4,8,16,4,80]{4,2,3,1,0:T(8,128)(2,1)} copy(bf16[4,8,16,4,80]{4,0,3,1,2:T(4,128)(2,1)S(1)} %bitcast.33) | data formatting | bytes 655360 | tf_op jit(solution)/shard_map/transpose | solution.py:74
  58.9 6.7 %all-to-all-start = ((bf16[32,16,4,80]{3,1,2,0:T(8,128)(2,1)}), bf16[32,16,4,80]{3,1,2,0:T(8,128)(2,1)S(1)}, u32[]{:S(2)}, u32[]{:S(2)}) async-start(bf16[32,16,4,80]{3,1,2,0:T(8,128)(2,1)} %bitcast.4), calls=%async_computation | async-start | bytes 1048576 | tf_op jit(solution)/shard_map/all_to_all | solution.py:75
  65.6 0.1 compare_select_fusion
  65.7 0.1 reshape.153
  65.8 0.0 copy-done.1
  65.8 0.0 copy-start.4
  65.8 0.0 copy-start.7
  65.8 1.9 %gather_fusion = s32[256]{0:T(256)S(1)} fusion(s32[128]{0:T(128)S(1)} %copy-done.1, s32[1024]{0:T(1024)S(1)} %pad_clamp_fusion.1), kind=kCustom, calls=%fused_computation | custom fusion | bytes 3072 | tf_op jit(solution)/shard_map/gather | solution.py:84
  67.7 0.1 reshape.152
  67.8 9.0 %all-to-all-done = bf16[32,16,4,80]{3,1,2,0:T(8,128)(2,1)S(1)} async-done(((bf16[32,16,4,80]{3,1,2,0:T(8,128)(2,1)}), bf16[32,16,4,80]{3,1,2,0:T(8,128)(2,1)S(1)}, u32[]{:S(2)}, u32[]{:S(2)}) %all-to-all-start) | async-done | bytes 327712 | tf_op jit(solution)/shard_map/all_to_all | solution.py:75
  76.8 0.1 convert_reduce_fusion
  76.9 0.1 copy.29
  77.0 0.0 copy-done.4
  77.0 0.0 copy-done.7
  77.0 0.9 %fusion.6 = bf16[4,64,80]{2,1,0:T(8,128)(2,1)} fusion(f32[4,64,80]{2,1,0:T(8,128)S(1)} %bitcast.35, bf16[4,64,80]{2,1,0:T(8,128)(2,1)S(1)} %copy-done.4, s32[4,64]{1,0:T(4,128)S(1)} %reshape.152, f32[50,80]{1,0:T(8,128)S(1)} %copy-done.7), kind=kOutput, calls=%fused_computation.12 | convolution fusion | flops 12382720 | bytes 180864 | tf_op jit(solution)/shard_map/tgs,sc->tgc/dot_general | solution.py:88
  (9 shorter events, 0.1 us)
Async XLA Ops:
  0.0 1.7 %copy-start = (bf16[16,16,640]{2,1,0:T(8,128)(2,1)S(1)}, bf16[16,16,640]{2,1,0:T(8,128)(2,1)}, u32[]{:S(2)}) copy-start(bf16[16,16,640]{2,1,0:T(8,128)(2,1)} %param.15) | copy-start | bytes 983044
  3.1 0.8 %copy-start.5 = (bf16[32,640]{1,0:T(8,128)(2,1)S(1)}, bf16[32,640]{1,0:T(8,128)(2,1)}, u32[]{:S(2)}) copy-start(bf16[32,640]{1,0:T(8,128)(2,1)} %param.12) | copy-start | bytes 122884
  3.1 1.0 %copy-start.2 = (bf16[16,16,640]{2,1,0:T(8,128)(2,1)S(1)}, bf16[16,16,640]{2,1,0:T(8,128)(2,1)}, u32[]{:S(2)}) copy-start(bf16[16,16,640]{2,1,0:T(8,128)(2,1)} %param.14) | copy-start | bytes 983044
  5.5 0.8 %copy-start.6 = (bf16[32,640]{1,0:T(8,128)(2,1)S(1)}, bf16[32,640]{1,0:T(8,128)(2,1)}, u32[]{:S(2)}) copy-start(bf16[32,640]{1,0:T(8,128)(2,1)} %param.11) | copy-start | bytes 122884
  5.5 0.8 %copy-start.8 = (s32[2]{0:T(128)S(1)}, s32[2]{0:T(128)}, u32[]{:S(2)}) copy-start(s32[2]{0:T(128)} %param.17) | copy-start | bytes 28
  6.9 34.1 %copy-start.3 = (bf16[640,80]{0,1:T(8,128)(2,1)S(1)}, bf16[640,80]{0,1:T(8,128)(2,1)}, u32[]{:S(2)}) copy-start(bf16[640,80]{0,1:T(8,128)(2,1)} %param.20) | copy-start | bytes 307204
  57.8 8.1 %copy-start.1 = (s32[128]{0:T(128)S(1)}, s32[128]{0:T(128)}, u32[]{:S(2)}) copy-start(s32[128]{0:T(128)} %param.18) | copy-start | bytes 1540
  58.9 17.9 %all-to-all-start = ((bf16[32,16,4,80]{3,1,2,0:T(8,128)(2,1)}), bf16[32,16,4,80]{3,1,2,0:T(8,128)(2,1)S(1)}, u32[]{:S(2)}, u32[]{:S(2)}) async-start(bf16[32,16,4,80]{3,1,2,0:T(8,128)(2,1)} %bitcast.4), calls=%async_computation | async-start | bytes 1048576 | tf_op jit(solution)/shard_map/all_to_all | solution.py:75
  65.8 11.2 %copy-start.4 = (bf16[4,64,80]{2,1,0:T(8,128)(2,1)S(1)}, bf16[4,64,80]{2,1,0:T(8,128)(2,1)}, u32[]{:S(2)}) copy-start(bf16[4,64,80]{2,1,0:T(8,128)(2,1)} %param.21) | copy-start | bytes 122884
  65.8 11.2 %copy-start.7 = (f32[50,80]{1,0:T(8,128)S(1)}, f32[50,80]{1,0:T(8,128)}, u32[]{:S(2)}) copy-start(f32[50,80]{1,0:T(8,128)} %param.19) | copy-start | bytes 48004
where the time goes:
time: 78.3 us; the launch traced here: 78 us
  blocking collectives  49.2 us (63%)
  local copies, waits for them, and re-layouts  9.44 us (12%)
  waiting for transfers between devices  9 us (11%)
  starting transfers between devices  6.69 us (9%)
  matrix products  2.42 us (3%)
  other arithmetic  0.98 us (1%)
    all_gather x1, blocking collectives, per_device(): attn_all = lax.all_gather(attn, 'z', axis=0, tiled=True)  33.5 us
    all_gather x1, blocking collectives, per_device(): weight = lax.all_gather(out_weight, ('y_hi', 'core'), axis=1, tiled=True)  15.7 us
    all_to_all x1, waiting for transfers between devices, per_device(): lax.all_to_all(blocks, ('y_hi', 'core', 'x', 'y_lo'), 0, 0, tiled=True)  9 us
    all_to_all x1, starting transfers between devices, per_device(): lax.all_to_all(blocks, ('y_hi', 'core', 'x', 'y_lo'), 0, 0, tiled=True)  6.69 us
    gather x2, local copies, waits for them, and re-layouts, per_device(): step_at = timesteps[request_at]  1.95 us
    concatenate x4, local copies, waits for them, and re-layouts, attend(): jnp.concatenate([value_pool[page_table].reshape(req_dev, cached, width),...  1.73 us
  transfers between devices with their start and end apart: 1, of which 1 were waited for; matrix products, arithmetic and copies ran while one was open for 3% of the time, Pallas kernels for 0%

commit v1 on v0

--- a/solution.py
+++ b/solution.py
@@ -66,7 +66,12 @@
     col_count = out_weight.shape[1]
     y_hi, z_len, cores = (lax.axis_size(name) for name in ("y_hi", "z", "core"))
     tensor_len = lax.axis_size("x") * lax.axis_size("y_lo")
-    weight = lax.all_gather(out_weight, ("y_hi", "core"), axis=1, tiled=True)
+    weight = jnp.concatenate(
+        lax.all_to_all(
+            jnp.stack([out_weight] * lax.axis_size(("y_hi", "core"))), ("y_hi", "core"), 0, 0
+        ),
+        axis=1,
+    )
     attn = attend(queries, new_keys, new_values, key_pool, value_pool, page_table, lengths)
     attn_all = lax.all_gather(attn, "z", axis=0, tiled=True)
     partial = jnp.dot(attn_all, weight, preferred_element_type=jnp.float32).astype(jnp.bfloat16)

time: 78.3 us -> 75 us (0.958)
  blocking collectives: 49.2 us -> 27.6 us
  starting transfers between devices: 6.69 us -> 24.7 us
  local copies, waits for them, and re-layouts: 9.44 us -> 10.3 us
    all_gather x1 -> x0, blocking collectives: 15.7 us -> none  [per_device(): weight = lax.all_gather(out_weight, ('y_hi', 'core'), axis=1, tiled=True)]
    all_to_all x0 -> x1, starting transfers between devices: none -> 10.3 us  [per_device(): lax.all_to_all(jnp.stack([out_weight] * lax.axis_size(('y_hi', 'core'))),...]
    all_to_all x1, starting transfers between devices: 6.69 us -> 14.5 us  [per_device(): lax.all_to_all(blocks, ('y_hi', 'core', 'x', 'y_lo'), 0, 0, tiled=True)]
    all_gather x1, blocking collectives: 33.5 us -> 27.6 us  [per_device(): attn_all = lax.all_gather(attn, 'z', axis=0, tiled=True)]
    another operation x0 -> x1, local copies, waits for them, and re-layouts: none -> 1.73 us  [per_device(): jnp.stack([out_weight] * lax.axis_size(('y_hi', 'core')))]
    concatenate x4, local copies, waits for them, and re-layouts: 1.73 us -> 0.9 us  [attend(): jnp.concatenate([value_pool[page_table].reshape(req_dev, cached, width),...]
  transfers between devices with their start and end apart: 1 -> 2, of which waited for: 1 -> 1; matrix products, arithmetic and copies ran while one was open for 3% -> 9% of each run, Pallas kernels for 0% -> 0%
where the time goes in v1:
time: 75 us; the launch traced here: 74.7 us
  blocking collectives  27.6 us (37%)
  starting transfers between devices  24.7 us (33%)
  local copies, waits for them, and re-layouts  10.3 us (14%)
  waiting for transfers between devices  9.04 us (12%)
  matrix products  2.43 us (3%)
    all_gather x1, blocking collectives, per_device(): attn_all = lax.all_gather(attn, 'z', axis=0, tiled=True)  27.6 us
    all_to_all x1, starting transfers between devices, per_device(): lax.all_to_all(blocks, ('y_hi', 'core', 'x', 'y_lo'), 0, 0, tiled=True)  14.5 us
    all_to_all x1, starting transfers between devices, per_device(): lax.all_to_all(jnp.stack([out_weight] * lax.axis_size(('y_hi', 'core'))),...  10.3 us
    all_to_all x1, waiting for transfers between devices, per_device(): lax.all_to_all(blocks, ('y_hi', 'core', 'x', 'y_lo'), 0, 0, tiled=True)  9.04 us
    gather x2, local copies, waits for them, and re-layouts, per_device(): step_at = timesteps[request_at]  1.95 us
    another operation x1, local copies, waits for them, and re-layouts, per_device(): jnp.stack([out_weight] * lax.axis_size(('y_hi', 'core')))  1.73 us
  transfers between devices with their start and end apart: 2, of which 1 were waited for; matrix products, arithmetic and copies ran while one was open for 9% of the time, Pallas kernels for 0%

profile of v1, /device:TPU:1, one launch (start us, length us, event | category | flops | bytes accessed | tf_op | source)
XLA Modules:
  0.0 74.7 jit_solution(7405348265615091282)
XLA Ops:
  0.0 0.0 copy-start
  0.0 0.0 copy-start.4
  0.0 0.0 copy-start.8
  0.0 1.7 %stack.2 = bf16[4,640,80]{1,2,0:T(8,128)(2,1)} broadcast(bf16[640,80]{0,1:T(8,128)(2,1)} %param.20), dimensions={1,2} | broadcast | bytes 512000 | tf_op jit(solution)/shard_map/stack | solution.py:71
  1.7 10.3 %all-to-all-start = ((bf16[4,640,80]{1,2,0:T(8,128)(2,1)}), bf16[4,640,80]{1,2,0:T(8,128)(2,1)S(1)}, u32[]{:S(2)}, u32[]{:S(2)}) async-start(bf16[4,640,80]{1,2,0:T(8,128)(2,1)} %stack.2), calls=%async_computation | async-start | bytes 819200 | tf_op jit(solution)/shard_map/all_to_all | solution.py:70
  12.0 0.0 copy-done.4
  12.0 0.1 concatenate.17
  12.1 0.0 copy-done.8
  12.1 0.1 reshape.171
  12.2 0.0 copy-done
  12.2 0.7 gather_fusion.1
  12.9 0.7 concatenate.16
  13.6 0.0 copy-start.5
  13.6 0.0 copy-start.2
  13.7 0.1 copy.22
  13.8 0.6 copy-done.5
  14.4 0.1 concatenate.20
  14.5 0.1 copy-done.2
  14.6 0.7 gather_fusion.2
  15.3 0.7 concatenate.19
  16.0 0.0 copy-start.6
  16.0 0.0 copy-start.9
  16.1 0.1 copy.24
  16.2 0.6 copy-done.6
  16.8 0.1 reshape.153
  16.9 0.0 copy-done.9
  16.9 0.1 compare_or_fusion
  17.0 0.5 fusion.48
  17.5 0.5 fusion.7
  18.1 27.6 %all_gather.3 = bf16[512,640]{1,0:T(8,128)(2,1)S(1)} all-gather(bf16[32,640]{1,0:T(8,128)(2,1)S(1)} %bitcast.41), channel_id=1, replica_groups=mesh['y_hi'=2,'z'=16,'core'=2,'x'=4,'y_lo'=2] {'z'}, dimensions={0}, use_global_device_ids=true | all-gather | bytes 696320 | tf_op jit(solution)/shard_map/all_gather | solution.py:76
  45.7 0.0 all-to-all-done
  45.7 0.4 convolution_convert_fusion
  46.1 0.2 copy.28
  46.3 0.3 reshape.157
  46.7 0.0 copy-start.1
  46.7 1.1 %copy.29 = bf16[4,8,16,4,80]{4,2,3,1,0:T(8,128)(2,1)} copy(bf16[4,8,16,4,80]{4,0,3,1,2:T(4,128)(2,1)S(1)} %bitcast.36) | data formatting | bytes 655360 | tf_op jit(solution)/shard_map/transpose | solution.py:79
  47.8 14.5 %all-to-all-start.1 = ((bf16[32,16,4,80]{3,1,2,0:T(8,128)(2,1)}), bf16[32,16,4,80]{3,1,2,0:T(8,128)(2,1)S(1)}, u32[]{:S(2)}, u32[]{:S(2)}) async-start(bf16[32,16,4,80]{3,1,2,0:T(8,128)(2,1)} %bitcast.6), calls=%async_computation.1 | async-start | bytes 1048576 | tf_op jit(solution)/shard_map/all_to_all | solution.py:80
  62.3 0.1 compare_select_fusion
  62.4 0.1 reshape.163
  62.5 0.0 copy-done.1
  62.5 0.0 copy-start.3
  62.5 0.0 copy-start.7
  62.5 1.9 %gather_fusion = s32[256]{0:T(256)S(1)} fusion(s32[128]{0:T(128)S(1)} %copy-done.1, s32[1024]{0:T(1024)S(1)} %pad_clamp_fusion.1), kind=kCustom, calls=%fused_computation | custom fusion | bytes 3072 | tf_op jit(solution)/shard_map/gather | solution.py:89
  64.4 0.1 reshape.162
  64.5 9.0 %all-to-all-done.1 = bf16[32,16,4,80]{3,1,2,0:T(8,128)(2,1)S(1)} async-done(((bf16[32,16,4,80]{3,1,2,0:T(8,128)(2,1)}), bf16[32,16,4,80]{3,1,2,0:T(8,128)(2,1)S(1)}, u32[]{:S(2)}, u32[]{:S(2)}) %all-to-all-start.1) | async-done | bytes 327712 | tf_op jit(solution)/shard_map/all_to_all | solution.py:80
  73.5 0.1 convert_reduce_fusion
  73.6 0.1 copy.30
  73.7 0.0 copy-done.3
  73.7 0.0 copy-done.7
  73.7 0.9 %fusion.6 = bf16[4,64,80]{2,1,0:T(8,128)(2,1)} fusion(f32[4,64,80]{2,1,0:T(8,128)S(1)} %bitcast.39, bf16[4,64,80]{2,1,0:T(8,128)(2,1)S(1)} %copy-done.3, s32[4,64]{1,0:T(4,128)S(1)} %reshape.162, f32[50,80]{1,0:T(8,128)S(1)} %copy-done.7), kind=kOutput, calls=%fused_computation.12 | convolution fusion | flops 12382720 | bytes 180864 | tf_op jit(solution)/shard_map/tgs,sc->tgc/dot_general | solution.py:93
  (10 shorter events, 0.1 us)
Async XLA Ops:
  0.0 12.2 %copy-start = (bf16[16,16,640]{2,1,0:T(8,128)(2,1)S(1)}, bf16[16,16,640]{2,1,0:T(8,128)(2,1)}, u32[]{:S(2)}) copy-start(bf16[16,16,640]{2,1,0:T(8,128)(2,1)} %param.15) | copy-start | bytes 983044
  0.0 12.0 %copy-start.4 = (bf16[32,640]{1,0:T(8,128)(2,1)S(1)}, bf16[32,640]{1,0:T(8,128)(2,1)}, u32[]{:S(2)}) copy-start(bf16[32,640]{1,0:T(8,128)(2,1)} %param.13) | copy-start | bytes 122884
  0.0 12.1 %copy-start.8 = (s32[2,16]{1,0:T(2,128)S(1)}, s32[2,16]{1,0:T(2,128)}, u32[]{:S(2)}) copy-start(s32[2,16]{1,0:T(2,128)} %param.16) | copy-start | bytes 388
  1.7 43.9 %all-to-all-start = ((bf16[4,640,80]{1,2,0:T(8,128)(2,1)}), bf16[4,640,80]{1,2,0:T(8,128)(2,1)S(1)}, u32[]{:S(2)}, u32[]{:S(2)}) async-start(bf16[4,640,80]{1,2,0:T(8,128)(2,1)} %stack.2), calls=%async_computation | async-start | bytes 819200 | tf_op jit(solution)/shard_map/all_to_all | solution.py:70
  13.6 0.8 %copy-start.5 = (bf16[32,640]{1,0:T(8,128)(2,1)S(1)}, bf16[32,640]{1,0:T(8,128)(2,1)}, u32[]{:S(2)}) copy-start(bf16[32,640]{1,0:T(8,128)(2,1)} %param.12) | copy-start | bytes 122884
  13.6 1.0 %copy-start.2 = (bf16[16,16,640]{2,1,0:T(8,128)(2,1)S(1)}, bf16[16,16,640]{2,1,0:T(8,128)(2,1)}, u32[]{:S(2)}) copy-start(bf16[16,16,640]{2,1,0:T(8,128)(2,1)} %param.14) | copy-start | bytes 983044
  16.0 0.8 %copy-start.6 = (bf16[32,640]{1,0:T(8,128)(2,1)S(1)}, bf16[32,640]{1,0:T(8,128)(2,1)}, u32[]{:S(2)}) copy-start(bf16[32,640]{1,0:T(8,128)(2,1)} %param.11) | copy-start | bytes 122884
  16.0 0.8 %copy-start.9 = (s32[2]{0:T(128)S(1)}, s32[2]{0:T(128)}, u32[]{:S(2)}) copy-start(s32[2]{0:T(128)} %param.17) | copy-start | bytes 28
  46.7 15.8 %copy-start.1 = (s32[128]{0:T(128)S(1)}, s32[128]{0:T(128)}, u32[]{:S(2)}) copy-start(s32[128]{0:T(128)} %param.18) | copy-start | bytes 1540
  47.8 25.7 %all-to-all-start.1 = ((bf16[32,16,4,80]{3,1,2,0:T(8,128)(2,1)}), bf16[32,16,4,80]{3,1,2,0:T(8,128)(2,1)S(1)}, u32[]{:S(2)}, u32[]{:S(2)}) async-start(bf16[32,16,4,80]{3,1,2,0:T(8,128)(2,1)} %bitcast.6), calls=%async_computation.1 | async-start | bytes 1048576 | tf_op jit(solution)/shard_map/all_to_all | solution.py:80
  62.5 11.2 %copy-start.3 = (bf16[4,64,80]{2,1,0:T(8,128)(2,1)S(1)}, bf16[4,64,80]{2,1,0:T(8,128)(2,1)}, u32[]{:S(2)}) copy-start(bf16[4,64,80]{2,1,0:T(8,128)(2,1)} %param.21) | copy-start | bytes 122884
  62.5 11.2 %copy-start.7 = (f32[50,80]{1,0:T(8,128)S(1)}, f32[50,80]{1,0:T(8,128)}, u32[]{:S(2)}) copy-start(f32[50,80]{1,0:T(8,128)} %param.19) | copy-start | bytes 48004
